TPU v7x, 32 devices: a whole 2x2x4 slice. The times are simulated.
32 devices in a mesh: wide: 16 (over z, y, x), narrow: 2 (over core).
Axes of the slice: x: 2, y: 2, z: 4, core: 2. Of those that a mesh axis runs over, the one named last changes fastest.
Arguments:
- x_trial: float32 [2, 512, 512], P(None, 'wide', 'narrow'), may hold values from -6 to 6
- psi_orb: float32 [512, 16384], P('narrow', 'wide'), may hold values from -0.046875 to 0.046875
- phi_orb: float32 [512, 16384], P('wide', 'narrow'), may hold values from -0.046875 to 0.046875
- screened: float32 [16384, 16384], P('wide', 'narrow'), may hold values from -192 to 192
- eps_val: float32 [512], P('wide'), may hold values from -1 to -0.1
- eps_cond: float32 [512], P('narrow'), may hold values from 0.1 to 1
Outputs:
- applied: float32 [2, 512, 512], P(None, 'wide', 'narrow')
All inputs are finite; a program needn't handle non-finite values.
Results may differ from a plain program's by a relative error of at most 0.00011.
Values sent between devices are 32-bit elements; how exact they have to be, the bound alone decides.
A program may use at most 192 MiB of HBM per device.

v0:
```python
import jax
import jax.numpy as jnp
from jax import lax
from jax.sharding import PartitionSpec as P


def local(x_trial, psi_orb, phi_orb, screened, eps_val, eps_cond):
    precise = lax.Precision.HIGHEST
    psi_rows = lax.all_gather(psi_orb, "narrow", axis=0, tiled=True)
    phi_cols = lax.all_gather(phi_orb, "wide", axis=0, tiled=True)
    x_cols = lax.all_gather(x_trial, "narrow", axis=2, tiled=True)
    x_whole = lax.all_gather(x_cols, "wide", axis=1, tiled=True)
    half_map = jnp.einsum("vr,tvc->trc", psi_rows, x_whole, precision=precise)
    pair_tile = jnp.einsum("trc,cs->trs", half_map, phi_cols, precision=precise) * screened[None]
    back_map = jnp.einsum("trs,cs->trc", pair_tile, phi_cols, precision=precise)
    summed = lax.psum_scatter(back_map, "narrow", scatter_dimension=2, tiled=True)
    val_part = jnp.einsum("vr,trc->tvc", psi_rows, summed, precision=precise)
    kernel = lax.psum_scatter(val_part, "wide", scatter_dimension=1, tiled=True)
    energy_gap = eps_cond[None, None, :] - eps_val[None, :, None]
    return kernel + energy_gap * x_trial


def solution(mesh):
    placed = (
        P(None, "wide", "narrow"),
        P("narrow", "wide"),
        P("wide", "narrow"),
        P("wide", "narrow"),
        P("wide"),
        P("narrow"),
    )
    return jax.shard_map(
        local, mesh=mesh, in_specs=placed, out_specs=P(None, "wide", "narrow"), check_vma=False
    )
```

profile of v0, /device:TPU:0, one launch (start us, length us, event | category | flops | bytes accessed | tf_op | source)
XLA Modules:
  0.0 646.4 jit_solution(13201375299929367361)
XLA Ops:
  6.5 0.7 all-gather.6.cloned.1.call-update
  7.3 0.0 all-gather.4.cloned.1.call-start
  7.3 3.7 all_gather.12
  11.0 0.0 all-gather.4.cloned.1.call-update
  11.0 0.0 all-gather.8.cloned.1.call-start
  11.1 0.7 all-gather.8.cloned.1.call-update
  11.8 0.0 reduce-scatter.2.cloned.1.call-start
  11.8 10.4 %all-gather.6.cloned.1.call-done = f32[512,1024]{1,0:T(8,128)} async-done(((f32[256,1024]{1,0:T(8,128)}), f32[512,1024]{1,0:T(8,128)}) %all-gather.6.cloned.1.call-update) | async-done | bytes 2097168 | tf_op jit(solution)/shard_map/all_gather | solution.py:9
  22.2 64.3 %all-gather.4.cloned.1.call-done = f32[2,512,512]{2,1,0:T(8,128)} async-done(((f32[2,32,512]{2,1,0:T(8,128)}), f32[2,512,512]{2,1,0:T(8,128)}) %all-gather.4.cloned.1.call-update) | async-done | bytes 2097168 | tf_op jit(solution)/shard_map/all_gather | solution.py:12
  86.5 10.3 %fusion.9 = f32[2,512,1024]{2,1,0:T(8,128)} fusion(f32[2,512,512]{2,1,0:T(8,128)} %all-gather.4.cloned.1.call-done, f32[512,1024]{1,0:T(8,128)} %all-gather.6.cloned.1.call-done), kind=kOutput, calls=%fused_computation.9 | convolution fusion | flops 6442450944 | bytes 8388608 | tf_op jit(solution)/shard_map/vr,tvc->trc/dot_general | solution.py:13
  96.8 182.3 %all-gather.8.cloned.1.call-done = f32[512,8192]{1,0:T(8,128)} async-done(((f32[32,8192]{1,0:T(8,128)}), f32[512,8192]{1,0:T(8,128)}) %all-gather.8.cloned.1.call-update) | async-done | bytes 16777232 | tf_op jit(solution)/shard_map/all_gather | solution.py:10
  279.0 112.7 %fusion.4 = f32[2,1024,8192]{2,1,0:T(8,128)} fusion(f32[512,8192]{1,0:T(8,128)} %all-gather.8.cloned.1.call-done, f32[2,512,1024]{2,1,0:T(8,128)} %fusion.9), kind=kOutput, calls=%fused_computation.4 | convolution fusion | flops 103079215104 | bytes 88080384 | tf_op jit(solution)/shard_map/trc,cs->trs/dot_general | solution.py:14
  391.8 112.9 %fusion = f32[2,1024,512]{2,1,0:T(8,128)} fusion(f32[2,1024,8192]{2,1,0:T(8,128)} %fusion.4, f32[1024,8192]{1,0:T(8,128)} %param.9, f32[512,8192]{1,0:T(8,128)} %all-gather.8.cloned.1.call-done), kind=kOutput, calls=%fused_computation | convolution fusion | flops 103095992320 | bytes 121634816 | tf_op jit(solution)/shard_map/trs,cs->trc/dot_general | solution.py:15
  504.7 0.0 reduce-scatter.2.cloned.1.call-update
  504.8 0.3 all-reduce.3.cloned.1.call-start
  505.1 9.9 %reduce-scatter.2.cloned.1.call-done = f32[2,1024,256]{2,1,0:T(8,128)} async-done(((f32[2,1024,512]{2,1,0:T(8,128)}), f32[2,1024,256]{2,1,0:T(8,128)}) %reduce-scatter.2.cloned.1.call-update) | async-done | bytes 2097168 | tf_op jit(solution)/shard_map/reduce_scatter | solution.py:16
  514.9 8.3 %fusion.11 = f32[2,512,256]{1,2,0:T(8,128)S(1)} fusion(f32[2,1024,256]{2,1,0:T(8,128)} %reduce-scatter.2.cloned.1.call-done, f32[512,1024]{1,0:T(8,128)S(1)} %copy-done), kind=kOutput, calls=%fused_computation.11 | convolution fusion | flops 3221225472 | bytes 5242880 | tf_op jit(solution)/shard_map/vr,trc->tvc/dot_general | solution.py:17
  523.2 1.3 copy.14
  524.5 0.0 all-reduce.3.cloned.1.call-update
  524.6 0.6 dynamic-slice
  525.8 0.1 broadcast_subtract_fusion
  525.9 112.5 %all-reduce.3.cloned.1.call-done = f32[2,512,256]{2,0,1:T(2,128)} async-done(((f32[2,512,256]{2,0,1:T(2,128)}), f32[2,512,256]{2,0,1:T(2,128)}) %all-reduce.3.cloned.1.call-update) | async-done | bytes 1048592
  638.4 0.8 constant_dynamic-slice_fusion
  639.2 0.6 copy_add_fusion
  (11 shorter events, 0.0 us)
Async XLA Ops:
  6.5 15.7 %all-gather.6.cloned.1.call-start = ((), (), s32[]{:S(2)}) async-start(), calls=%async_computation.2 | async-start | bytes 3145728 | tf_op jit(solution)/shard_map/all_gather | solution.py:9
  7.3 79.2 %all-gather.4.cloned.1.call-start = ((), (), s32[]{:S(2)}) async-start(), calls=%async_computation.1 | async-start | bytes 2228224 | tf_op jit(solution)/shard_map/all_gather | solution.py:12
  11.0 268.0 %all-gather.8.cloned.1.call-start = ((), (), s32[]{:S(2)}) async-start(), calls=%async_computation.3 | async-start | bytes 17825792 | tf_op jit(solution)/shard_map/all_gather | solution.py:10
  11.8 503.1 %reduce-scatter.2.cloned.1.call-start = ((), (), s32[]{:S(2)}) async-start(), calls=%async_computation.4 | async-start | bytes 6291456 | tf_op jit(solution)/shard_map/reduce_scatter | solution.py:16
  504.7 10.2 %copy-start = (f32[512,1024]{1,0:T(8,128)S(1)}, f32[512,1024]{1,0:T(8,128)}, u32[]{:S(2)}) copy-start(f32[512,1024]{1,0:T(8,128)} %all-gather.6.cloned.1.call-done) | copy-start | bytes 6291460
  504.7 19.9 %copy-start.4 = (u32[32]{0:T(128)S(1)}, u32[32]{0:T(128)}, u32[]{:S(2)}) copy-start(u32[32]{0:T(128)} %constant.2) | copy-start | bytes 388
  504.7 21.1 %copy-start.2 = (f32[256]{0:T(256)S(1)}, f32[256]{0:T(256)}, u32[]{:S(2)}) copy-start(f32[256]{0:T(256)} %param.11) | copy-start | bytes 3076
  504.7 21.1 %copy-start.3 = (f32[32]{0:T(128)S(1)}, f32[32]{0:T(128)}, u32[]{:S(2)}) copy-start(f32[32]{0:T(128)} %param.10) | copy-start | bytes 388
  504.7 134.5 %copy-start.1 = (f32[2,32,256]{2,1,0:T(8,128)S(1)}, f32[2,32,256]{2,1,0:T(8,128)}, u32[]{:S(2)}) copy-start(f32[2,32,256]{2,1,0:T(8,128)} %param.6) | copy-start | bytes 196612
  504.8 133.6 %all-reduce.3.cloned.1.call-start = ((), (), s32[]{:S(2)}) async-start(), calls=%async_computation.5 | async-start | bytes 2097152
Sparse Core Ops, SparseCore 0:
  8.9 13.2 all-gather.5
  25.0 61.4 all-gather.3
  89.3 189.7 all-gather.7
  504.8 10.0 reduce-scatter.1
  524.7 113.6 all-reduce.2
where the time goes:
time: 647 us; the launch traced here: 646 us
  waiting for transfers between devices  381 us (59%)
  matrix products  244 us (38%)
  between operations  13.9 us (2%)
    all_gather x1, waiting for transfers between devices, local(): phi_cols = lax.all_gather(phi_orb, 'wide', axis=0, tiled=True)  182 us
    unnamed x6, waiting for transfers between devices  114 us
    dot_general x1, matrix products, local(): back_map = jnp.einsum('trs,cs->trc', pair_tile, phi_cols, precision=precise)  113 us
    dot_general x1, matrix products, local(): jnp.einsum('trc,cs->trs', half_map, phi_cols, precision=precise)  113 us
    all_gather x1, waiting for transfers between devices, local(): x_whole = lax.all_gather(x_cols, 'wide', axis=1, tiled=True)  64.3 us
  transfers between devices with their start and end apart: 5, of which 5 were waited for; matrix products, arithmetic and copies ran while one was open for 2% of the time, Pallas kernels for 0%

commit v1 on v0

--- a/solution.py
+++ b/solution.py
@@ -9,8 +9,37 @@
     psi_rows = lax.all_gather(psi_orb, "narrow", axis=0, tiled=True)
     phi_cols = lax.all_gather(phi_orb, "wide", axis=0, tiled=True)
     x_cols = lax.all_gather(x_trial, "narrow", axis=2, tiled=True)
-    x_whole = lax.all_gather(x_cols, "wide", axis=1, tiled=True)
-    half_map = jnp.einsum("vr,tvc->trc", psi_rows, x_whole, precision=precise)
+    size, here, span = (lax.axis_size("wide"), lax.axis_index("wide"), x_cols.shape[1])
+    right = [(i, (i + 1) % size) for i in range(size)]
+    left = [(i, (i - 1) % size) for i in range(size)]
+    half = size // 2
+    from_left = from_right = x_cols
+    half_map = jnp.einsum(
+        "vr,tvc->trc",
+        lax.dynamic_slice_in_dim(psi_rows, here * span, x_cols.shape[1], axis=0),
+        x_cols,
+        precision=precise,
+    )
+    for step in range(1, half + 1):
+        from_left = lax.ppermute(from_left, "wide", right)
+        if step < size - half:
+            from_right = lax.ppermute(from_right, "wide", left)
+            half_map = half_map + jnp.einsum(
+                "vr,tvc->trc",
+                lax.dynamic_slice_in_dim(
+                    psi_rows, (here + step) % size * span, from_right.shape[1], axis=0
+                ),
+                from_right,
+                precision=precise,
+            )
+        half_map = half_map + jnp.einsum(
+            "vr,tvc->trc",
+            lax.dynamic_slice_in_dim(
+                psi_rows, (here - step) % size * span, from_left.shape[1], axis=0
+            ),
+            from_left,
+            precision=precise,
+        )
     pair_tile = jnp.einsum("trc,cs->trs", half_map, phi_cols, precision=precise) * screened[None]
     back_map = jnp.einsum("trs,cs->trc", pair_tile, phi_cols, precision=precise)
     summed = lax.psum_scatter(back_map, "narrow", scatter_dimension=2, tiled=True)

time: 647 us -> 633 us (0.978); the launches traced: 646 us -> 624 us
  waiting for transfers between devices: 381 us -> 215 us
  matrix products: 244 us -> 345 us
  starting transfers between devices: 0.42 us -> 43 us
    all_gather x1, waiting for transfers between devices: 182 us -> 59.3 us  [local(): phi_cols = lax.all_gather(phi_orb, 'wide', axis=0, tiled=True)]
    dot_general x1 -> x16, matrix products: 10.3 us -> 84.2 us  [the longest x8 42.7 us: local(): jnp.einsum('vr,tvc->trc', lax.dynamic_slice_in_dim(psi_rows, (here - step...]
    all_gather x1 -> x0, waiting for transfers between devices: 64.3 us -> none  [local(): x_whole = lax.all_gather(x_cols, 'wide', axis=1, tiled=True)]
    ppermute x0 -> x15, starting transfers between devices: none -> 42.6 us  [the longest x7 39.7 us: local(): from_right = lax.ppermute(from_right, 'wide', left)]
    ppermute x0 -> x15, waiting for transfers between devices: none -> 32.2 us  [the longest x8 24.6 us: local(): from_left = lax.ppermute(from_left, 'wide', right)]
    dot_general x1, matrix products: 113 us -> 140 us  [local(): jnp.einsum('trc,cs->trs', half_map, phi_cols, precision=precise)]
    all_gather x1, waiting for transfers between devices: 10.4 us -> 0.02 us  [local(): psi_rows = lax.all_gather(psi_orb, 'narrow', axis=0, tiled=True)]
    unnamed x6 -> x5, waiting for transfers between devices: 114 us -> 114 us
  transfers between devices with their start and end apart: 5 -> 19, of which waited for: 5 -> 14; matrix products, arithmetic and copies ran while one was open for 2% -> 14% of each run, Pallas kernels for 0% -> 0%
where the time goes in v1:
time: 633 us; the launch traced here: 624 us
  matrix products  345 us (55%)
  waiting for transfers between devices  215 us (34%)
  starting transfers between devices  43 us (7%)
  between operations  14.4 us (2%)
    dot_general x1, matrix products, local(): jnp.einsum('trc,cs->trs', half_map, phi_cols, precision=precise)  140 us
    unnamed x5, waiting for transfers between devices  114 us
    dot_general x1, matrix products, local(): back_map = jnp.einsum('trs,cs->trc', pair_tile, phi_cols, precision=precise)  113 us
    all_gather x1, waiting for transfers between devices, local(): phi_cols = lax.all_gather(phi_orb, 'wide', axis=0, tiled=True)  59.3 us
    dot_general x8, matrix products, local(): jnp.einsum('vr,tvc->trc', lax.dynamic_slice_in_dim(psi_rows, (here - step...  42.7 us
    ppermute x7, starting transfers between devices, local(): from_right = lax.ppermute(from_right, 'wide', left)  39.7 us
    dot_general x7, matrix products, local(): jnp.einsum('vr,tvc->trc', lax.dynamic_slice_in_dim(psi_rows, (here + step...  36.5 us
    ppermute x8, waiting for transfers between devices, local(): from_left = lax.ppermute(from_left, 'wide', right)  24.6 us
  transfers between devices with their start and end apart: 19, of which 14 were waited for; matrix products, arithmetic and copies ran while one was open for 14% of the time, Pallas kernels for 0%

profile of v1, /device:TPU:0, one launch (start us, length us, event | category | flops | bytes accessed | tf_op | source)
XLA Modules:
  0.0 623.6 jit_solution(12701375967152622295)
XLA Ops:
  21.0 5.6 collective-permute-start.2
  29.6 5.6 collective-permute-start.4
  40.4 6.1 collective-permute-start.6
  52.1 6.1 collective-permute-start.8
  64.3 6.1 collective-permute-start.10
  73.2 6.1 collective-permute-start.12
  79.3 5.7 collective-permute-done.13
  85.1 6.1 fusion.29
  91.2 5.1 fusion.33
  101.4 5.1 fusion.37
  106.5 5.1 fusion.39
  111.7 5.1 fusion.41
  116.7 5.1 fusion.43
  121.8 5.1 fusion.45
  126.9 5.3 fusion.47
  142.3 5.1 fusion.53
  157.4 5.9 fusion.31
  163.4 6.0 fusion.27
  169.4 59.3 %all-gather.5.cloned.1.call-done = f32[512,8192]{1,0:T(8,128)} async-done(((f32[32,8192]{1,0:T(8,128)}), f32[512,8192]{1,0:T(8,128)}) %all-gather.5.cloned.1.call-update) | async-done | bytes 16777232 | tf_op jit(solution)/shard_map/all_gather | solution.py:10
  228.6 139.6 %fusion.4 = f32[2,1024,8192]{2,1,0:T(8,128)} fusion(f32[512,8192]{1,0:T(8,128)} %all-gather.5.cloned.1.call-done, f32[1024,2,512]{2,0,1:T(8,128)} %fusion.27, f32[1024,2,512]{2,0,1:T(8,128)} %fusion.29, f32[1024,2,512]{2,0,1:T(8,128)} %fusion.31, f32[1024,2,512]{2,0,1:T(8,128)} %fusion.33, f32[1024,2,512]{2,0,1:T(8,128)} %fusion.35, ...), kind=kOutput, calls=%fused_computation.4 | convolution fusion | flops 103094943744 | bytes 150994944 | tf_op jit(solution)/shard_map/trc,cs->trs/dot_general | solution.py:43
  368.2 113.1 %fusion = f32[2,1024,512]{2,1,0:T(8,128)} fusion(f32[2,1024,8192]{2,1,0:T(8,128)} %fusion.4, f32[1024,8192]{1,0:T(8,128)} %param.9, f32[512,8192]{1,0:T(8,128)} %all-gather.5.cloned.1.call-done), kind=kOutput, calls=%fused_computation | convolution fusion | flops 103095992320 | bytes 121634816 | tf_op jit(solution)/shard_map/trs,cs->trc/dot_general | solution.py:44
  481.8 9.8 %reduce-scatter.2.cloned.1.call-done = f32[2,1024,256]{2,1,0:T(8,128)} async-done(((f32[2,1024,512]{2,1,0:T(8,128)}), f32[2,1024,256]{2,1,0:T(8,128)}) %reduce-scatter.2.cloned.1.call-update) | async-done | bytes 2097168 | tf_op jit(solution)/shard_map/reduce_scatter | solution.py:45
  491.6 8.3 %fusion.24 = f32[2,512,256]{1,2,0:T(8,128)S(1)} fusion(f32[2,1024,256]{2,1,0:T(8,128)} %reduce-scatter.2.cloned.1.call-done, f32[512,1024]{1,0:T(8,128)S(1)} %copy-done), kind=kOutput, calls=%fused_computation.24 | convolution fusion | flops 3221225472 | bytes 5242880 | tf_op jit(solution)/shard_map/vr,trc->tvc/dot_general | solution.py:46
  502.6 112.5 %all-reduce.3.cloned.1.call-done = f32[2,512,256]{2,0,1:T(2,128)} async-done(((f32[2,512,256]{2,0,1:T(2,128)}), f32[2,512,256]{2,0,1:T(2,128)}) %all-reduce.3.cloned.1.call-update) | async-done | bytes 1048592
  (65 shorter events, 66.2 us)
Async XLA Ops:
  6.5 78.5 %all-gather.3.cloned.1.call-start = ((), (), s32[]{:S(2)}) async-start(), calls=%async_computation.1 | async-start | bytes 3145728 | tf_op jit(solution)/shard_map/all_gather | solution.py:9
  7.3 221.4 %all-gather.5.cloned.1.call-start = ((), (), s32[]{:S(2)}) async-start(), calls=%async_computation.2 | async-start | bytes 17825792 | tf_op jit(solution)/shard_map/all_gather | solution.py:10
  8.0 483.6 %reduce-scatter.2.cloned.1.call-start = ((), (), s32[]{:S(2)}) async-start(), calls=%async_computation.3 | async-start | bytes 6291456 | tf_op jit(solution)/shard_map/reduce_scatter | solution.py:45
  10.3 10.7 %collective-permute-start.1 = (f32[2,32,512]{2,1,0:T(8,128)S(1)}, f32[2,32,512]{2,1,0:T(8,128)S(1)}, u32[]{:S(2)}, u32[]{:S(2)}) collective-permute-start(f32[2,32,512]{2,1,0:T(8,128)S(1)} %all_gather.10), channel_id=1, source_target_pairs={{0,2},{2,4},{4,6},{6,8},{8,10},{10,12},{12,14},{14,16},{16,18},{18... | collective-permute-start | bytes 393224 | tf_op jit(solution)/shard_map/ppermute | solution.py:24
  13.1 7.9 %collective-permute-start = (f32[2,32,512]{2,1,0:T(8,128)S(1)}, f32[2,32,512]{2,1,0:T(8,128)S(1)}, u32[]{:S(2)}, u32[]{:S(2)}) collective-permute-start(f32[2,32,512]{2,1,0:T(8,128)S(1)} %all_gather.10), channel_id=1, source_target_pairs={{0,30},{2,0},{4,2},{6,4},{8,6},{10,8},{12,10},{14,12},{16,14},{18,... | collective-permute-start | bytes 393224 | tf_op jit(solution)/shard_map/ppermute | solution.py:26
  21.0 8.6 %collective-permute-start.3 = (f32[2,32,512]{2,1,0:T(8,128)S(1)}, f32[2,32,512]{2,1,0:T(8,128)S(1)}, u32[]{:S(2)}, u32[]{:S(2)}) collective-permute-start(f32[2,32,512]{2,1,0:T(8,128)S(1)} %collective-permute-done.1), channel_id=1, source_target_pairs={{0,2},{2,4},{4,6},{6,8},{8,10},{10,12},{12,14},{14,16},{16,18},{18... | collective-permute-start | bytes 393224 | tf_op jit(solution)/shard_map/ppermute | solution.py:24
  21.0 8.6 %collective-permute-start.2 = (f32[2,32,512]{2,1,0:T(8,128)S(1)}, f32[2,32,512]{2,1,0:T(8,128)S(1)}, u32[]{:S(2)}, u32[]{:S(2)}) collective-permute-start(f32[2,32,512]{2,1,0:T(8,128)S(1)} %collective-permute-done), channel_id=1, source_target_pairs={{0,30},{2,0},{4,2},{6,4},{8,6},{10,8},{12,10},{14,12},{16,14},{18,... | collective-permute-start | bytes 393224 | tf_op jit(solution)/shard_map/ppermute | solution.py:26
  29.6 8.7 %collective-permute-start.5 = (f32[2,32,512]{2,1,0:T(8,128)S(1)}, f32[2,32,512]{2,1,0:T(8,128)S(1)}, u32[]{:S(2)}, u32[]{:S(2)}) collective-permute-start(f32[2,32,512]{2,1,0:T(8,128)S(1)} %collective-permute-done.3), channel_id=1, source_target_pairs={{0,2},{2,4},{4,6},{6,8},{8,10},{10,12},{12,14},{14,16},{16,18},{18... | collective-permute-start | bytes 393224 | tf_op jit(solution)/shard_map/ppermute | solution.py:24
  29.6 10.8 %collective-permute-start.4 = (f32[2,32,512]{2,1,0:T(8,128)S(1)}, f32[2,32,512]{2,1,0:T(8,128)S(1)}, u32[]{:S(2)}, u32[]{:S(2)}) collective-permute-start(f32[2,32,512]{2,1,0:T(8,128)S(1)} %collective-permute-done.2), channel_id=1, source_target_pairs={{0,30},{2,0},{4,2},{6,4},{8,6},{10,8},{12,10},{14,12},{16,14},{18,... | collective-permute-start | bytes 393224 | tf_op jit(solution)/shard_map/ppermute | solution.py:26
  38.3 11.5 %collective-permute-start.7 = (f32[2,32,512]{2,1,0:T(8,128)S(1)}, f32[2,32,512]{2,1,0:T(8,128)S(1)}, u32[]{:S(2)}, u32[]{:S(2)}) collective-permute-start(f32[2,32,512]{2,1,0:T(8,128)S(1)} %collective-permute-done.5), channel_id=1, source_target_pairs={{0,2},{2,4},{4,6},{6,8},{8,10},{10,12},{12,14},{14,16},{16,18},{18... | collective-permute-start | bytes 393224 | tf_op jit(solution)/shard_map/ppermute | solution.py:24
  40.4 11.7 %collective-permute-start.6 = (f32[2,32,512]{2,1,0:T(8,128)S(1)}, f32[2,32,512]{2,1,0:T(8,128)S(1)}, u32[]{:S(2)}, u32[]{:S(2)}) collective-permute-start(f32[2,32,512]{2,1,0:T(8,128)S(1)} %collective-permute-done.4), channel_id=1, source_target_pairs={{0,30},{2,0},{4,2},{6,4},{8,6},{10,8},{12,10},{14,12},{16,14},{18,... | collective-permute-start | bytes 393224 | tf_op jit(solution)/shard_map/ppermute | solution.py:26
  49.8 11.5 %collective-permute-start.9 = (f32[2,32,512]{2,1,0:T(8,128)S(1)}, f32[2,32,512]{2,1,0:T(8,128)S(1)}, u32[]{:S(2)}, u32[]{:S(2)}) collective-permute-start(f32[2,32,512]{2,1,0:T(8,128)S(1)} %collective-permute-done.7), channel_id=1, source_target_pairs={{0,2},{2,4},{4,6},{6,8},{8,10},{10,12},{12,14},{14,16},{16,18},{18... | collective-permute-start | bytes 393224 | tf_op jit(solution)/shard_map/ppermute | solution.py:24
  52.1 12.2 %collective-permute-start.8 = (f32[2,32,512]{2,1,0:T(8,128)S(1)}, f32[2,32,512]{2,1,0:T(8,128)S(1)}, u32[]{:S(2)}, u32[]{:S(2)}) collective-permute-start(f32[2,32,512]{2,1,0:T(8,128)S(1)} %collective-permute-done.6), channel_id=1, source_target_pairs={{0,30},{2,0},{4,2},{6,4},{8,6},{10,8},{12,10},{14,12},{16,14},{18,... | collective-permute-start | bytes 393224 | tf_op jit(solution)/shard_map/ppermute | solution.py:26
  61.3 11.6 %collective-permute-start.11 = (f32[2,32,512]{2,1,0:T(8,128)S(1)}, f32[2,32,512]{2,1,0:T(8,128)S(1)}, u32[]{:S(2)}, u32[]{:S(2)}) collective-permute-start(f32[2,32,512]{2,1,0:T(8,128)S(1)} %collective-permute-done.9), channel_id=1, source_target_pairs={{0,2},{2,4},{4,6},{6,8},{8,10},{10,12},{12,14},{14,16},{16,18},{18... | collective-permute-start | bytes 393224 | tf_op jit(solution)/shard_map/ppermute | solution.py:24
  64.3 20.8 %copy-start.4 = (f32[2,32,512]{2,1,0:T(8,128)}, f32[2,32,512]{2,1,0:T(8,128)S(1)}, u32[]{:S(2)}) copy-start(f32[2,32,512]{2,1,0:T(8,128)S(1)} %collective-permute-done.8) | copy-start | bytes 393220
  64.3 8.9 %collective-permute-start.10 = (f32[2,32,512]{2,1,0:T(8,128)S(1)}, f32[2,32,512]{2,1,0:T(8,128)S(1)}, u32[]{:S(2)}, u32[]{:S(2)}) collective-permute-start(f32[2,32,512]{2,1,0:T(8,128)S(1)} %collective-permute-done.8), channel_id=1, source_target_pairs={{0,30},{2,0},{4,2},{6,4},{8,6},{10,8},{12,10},{14,12},{16,14},{18,... | collective-permute-start | bytes 393224 | tf_op jit(solution)/shard_map/ppermute | solution.py:26
  72.9 12.1 %collective-permute-start.13 = (f32[2,32,512]{2,1,0:T(8,128)S(1)}, f32[2,32,512]{2,1,0:T(8,128)S(1)}, u32[]{:S(2)}, u32[]{:S(2)}) collective-permute-start(f32[2,32,512]{2,1,0:T(8,128)S(1)} %collective-permute-done.11), channel_id=1, source_target_pairs={{0,2},{2,4},{4,6},{6,8},{8,10},{10,12},{12,14},{14,16},{16,18},{18... | collective-permute-start | bytes 393224 | tf_op jit(solution)/shard_map/ppermute | solution.py:24
  73.2 84.3 %collective-permute-start.12 = (f32[2,32,512]{2,1,0:T(8,128)S(1)}, f32[2,32,512]{2,1,0:T(8,128)}, u32[]{:S(2)}, u32[]{:S(2)}) collective-permute-start(f32[2,32,512]{2,1,0:T(8,128)S(1)} %collective-permute-done.10), channel_id=1, source_target_pairs={{0,30},{2,0},{4,2},{6,4},{8,6},{10,8},{12,10},{14,12},{16,14},{18,... | collective-permute-start | bytes 393224 | tf_op jit(solution)/shard_map/ppermute | solution.py:26
  85.0 78.3 %collective-permute-start.14 = (f32[2,32,512]{2,1,0:T(8,128)S(1)}, f32[2,32,512]{2,1,0:T(8,128)}, u32[]{:S(2)}, u32[]{:S(2)}) collective-permute-start(f32[2,32,512]{2,1,0:T(8,128)S(1)} %collective-permute-done.13), channel_id=1, source_target_pairs={{0,2},{2,4},{4,6},{6,8},{8,10},{10,12},{12,14},{14,16},{16,18},{18... | collective-permute-start | bytes 393224 | tf_op jit(solution)/shard_map/ppermute | solution.py:24
  481.4 19.8 %copy-start.10 = (u32[32]{0:T(128)S(1)}, u32[32]{0:T(128)}, u32[]{:S(2)}) copy-start(u32[32]{0:T(128)} %constant.113) | copy-start | bytes 388
  481.4 21.1 %copy-start.8 = (f32[256]{0:T(256)S(1)}, f32[256]{0:T(256)}, u32[]{:S(2)}) copy-start(f32[256]{0:T(256)} %param.11) | copy-start | bytes 3076
  481.4 21.1 %copy-start.9 = (f32[32]{0:T(128)S(1)}, f32[32]{0:T(128)}, u32[]{:S(2)}) copy-start(f32[32]{0:T(128)} %param.10) | copy-start | bytes 388
  481.5 134.5 %copy-start.1 = (f32[2,32,256]{2,1,0:T(8,128)S(1)}, f32[2,32,256]{2,1,0:T(8,128)}, u32[]{:S(2)}) copy-start(f32[2,32,256]{2,1,0:T(8,128)} %param.6) | copy-start | bytes 196612
  481.5 133.6 %all-reduce.3.cloned.1.call-start = ((), (), s32[]{:S(2)}) async-start(), calls=%async_computation.4 | async-start | bytes 2097152
  (6 other events, 53.8 us)
Sparse Core Ops, SparseCore 0:
  8.9 13.2 all-gather.2
  25.0 203.6 all-gather.4
  481.5 10.0 reduce-scatter.1
  501.4 113.6 all-reduce.2
